TPU v7x, 512 devices: a whole 4x8x8 slice. The times are simulated.
512 devices in a mesh: dp: 128 (over y, z, core), rep: 4 (over x).
Axes of the slice: x: 4, y: 8, z: 8, core: 2. Of those that a mesh axis runs over, the one named last changes fastest.
Arguments:
- gradient_receptance: bfloat16 [128, 4, 2, 768, 768], P('dp', 'rep'), may hold values from -1000 to 1000
- gradient_factors: bfloat16 [128, 4, 2, 768, 256], P('dp', 'rep'), may hold values from -1000 to 1000
- gradient_channels: bfloat16 [128, 4, 2, 768, 16], P('dp', 'rep'), may hold values from -1000 to 1000
- primary_receptance: float32 [768, 768], P('dp'), may hold values from -0.21875 to 0.21875
- primary_factors: float32 [768, 256], P('dp'), may hold values from -0.21875 to 0.21875
- primary_channels: float32 [768, 16], P('dp'), may hold values from -1 to 1
- first_moment_receptance: float32 [768, 768], P('dp'), may hold values from -0.00390625 to 0.00390625
- first_moment_factors: float32 [768, 256], P('dp'), may hold values from -0.00390625 to 0.00390625
- first_moment_channels: float32 [768, 16], P('dp'), may hold values from -0.00390625 to 0.00390625
- second_moment_receptance: float32 [768, 768], P('dp'), may hold values from 1e-08 to 1e-06
- second_moment_factors: float32 [768, 256], P('dp'), may hold values from 1e-08 to 1e-06
- second_moment_channels: float32 [768, 16], P('dp'), may hold values from 1e-08 to 1e-06
Outputs:
- weight_receptance: bfloat16 [768, 768], replicated
- weight_lora: bfloat16 [768, 256], replicated
- weight_vectors: bfloat16 [768, 16], replicated
- new_master_receptance: float32 [768, 768], P('dp')
- new_master_lora: float32 [768, 256], P('dp')
- new_master_vectors: float32 [768, 16], P('dp')
- new_first_receptance: float32 [768, 768], P('dp')
- new_first_lora: float32 [768, 256], P('dp')
- new_first_vectors: float32 [768, 16], P('dp')
- new_second_receptance: float32 [768, 768], P('dp')
- new_second_lora: float32 [768, 256], P('dp')
- new_second_vectors: float32 [768, 16], P('dp')
All inputs are finite; a program needn't handle non-finite values.
Results may differ from a plain program's by a relative error of at most 0.001.
Values may be sent and summed in bfloat16 or wider, within the bound.
A program may use at most 64 MiB of HBM per device.

v0:
```python
import jax
import jax.numpy as jnp
from jax import lax
from jax.sharding import PartitionSpec as P

STEP = 20
beta_one = 0.9
beta_two = 0.99
adam_eps = 1e-08
learn_rate = 0.001
weight_decay_rate = 0.1
max_norm = 1.0
norm_eps = 1e-06


def decoupled_adam_step(gradient, master, first, second, decay):
    new_first = beta_one * first + (1.0 - beta_one) * gradient
    new_second = beta_two * second + (1.0 - beta_two) * gradient * gradient
    update = (
        new_first
        / (1.0 - beta_one**STEP)
        / (jnp.sqrt(new_second / (1.0 - beta_two**STEP)) + adam_eps)
    )
    new_master = master - learn_rate * (update + decay * master)
    return (new_master, new_first, new_second)


def body(
    gradient_receptance,
    gradient_factors,
    gradient_channels,
    primary_receptance,
    primary_factors,
    primary_channels,
    first_moment_receptance,
    first_moment_factors,
    first_moment_channels,
    second_moment_receptance,
    second_moment_factors,
    second_moment_channels,
):
    row_count = primary_receptance.shape[0]
    receptance_width = primary_receptance.shape[1]
    factor_width = primary_factors.shape[1]
    local_sum = jnp.concatenate(
        [
            jnp.sum(gradient_receptance, axis=(0, 1, 2), dtype=jnp.float32),
            jnp.sum(gradient_factors, axis=(0, 1, 2), dtype=jnp.float32),
            jnp.sum(gradient_channels, axis=(0, 1, 2), dtype=jnp.float32),
        ],
        axis=1,
    )
    full_sum = lax.psum(local_sum, ("dp", "rep"))
    square_sum = jnp.sum(full_sum * full_sum)
    owned_rows = lax.dynamic_slice_in_dim(full_sum, lax.axis_index("dp") * row_count, row_count, 0)
    clipping_ratio = jnp.minimum(1.0, max_norm / (jnp.sqrt(square_sum) + norm_eps))
    gradient_clipped = clipping_ratio * owned_rows
    separate_factors = receptance_width + factor_width
    receptance_part = decoupled_adam_step(
        gradient_clipped[:, :receptance_width],
        primary_receptance,
        first_moment_receptance,
        second_moment_receptance,
        weight_decay_rate,
    )
    lowrank_factors = decoupled_adam_step(
        gradient_clipped[:, receptance_width:separate_factors],
        primary_factors,
        first_moment_factors,
        second_moment_factors,
        weight_decay_rate,
    )
    channel_vectors = decoupled_adam_step(
        gradient_clipped[:, separate_factors:],
        primary_channels,
        first_moment_channels,
        second_moment_channels,
        0.0,
    )
    packed_gradients = jnp.concatenate(
        [receptance_part[0], lowrank_factors[0], channel_vectors[0]], axis=1
    ).astype(jnp.bfloat16)
    collected_parts = lax.all_gather(packed_gradients, "dp", axis=0, tiled=True)
    return (
        collected_parts[:, :receptance_width],
        collected_parts[:, receptance_width:separate_factors],
        collected_parts[:, separate_factors:],
        receptance_part[0],
        lowrank_factors[0],
        channel_vectors[0],
        receptance_part[1],
        lowrank_factors[1],
        channel_vectors[1],
        receptance_part[2],
        lowrank_factors[2],
        channel_vectors[2],
    )


def solution(mesh):
    placed = (
        P("dp", "rep", None, None, None),
        P("dp", "rep", None, None, None),
        P("dp", "rep", None, None, None),
        P("dp", None),
        P("dp", None),
        P("dp", None),
        P("dp", None),
        P("dp", None),
        P("dp", None),
        P("dp", None),
        P("dp", None),
        P("dp", None),
    )
    return jax.shard_map(
        body,
        mesh=mesh,
        in_specs=placed,
        out_specs=(
            P(),
            P(),
            P(),
            P("dp", None),
            P("dp", None),
            P("dp", None),
            P("dp", None),
            P("dp", None),
            P("dp", None),
            P("dp", None),
            P("dp", None),
            P("dp", None),
        ),
        check_vma=False,
    )
```

profile of v0, /device:TPU:1, one launch (start us, length us, event | category | flops | bytes accessed | tf_op | source)
XLA Modules:
  0.0 402.7 jit_solution(3003062648250207814)
XLA Ops:
  7.2 0.0 all-reduce.2.cloned.1.call-start
  7.2 0.8 convert_reduce_fusion.2
  8.0 0.2 copy.26
  8.2 1.3 convert_reduce_fusion.1
  9.5 2.3 convert_reduce_fusion
  11.9 2.0 pad_maximum_fusion
  13.9 0.0 copy-start.4
  13.9 0.0 copy-start
  13.9 0.0 copy-start.1
  14.0 0.0 all-reduce.2.cloned.1.call-update
  14.0 0.0 all-gather.3.cloned.1.call-start
  14.1 288.3 %all-reduce.2.cloned.1.call-done = f32[768,1040]{1,0:T(8,128)} async-done(((f32[768,1040]{1,0:T(8,128)}), f32[768,1040]{1,0:T(8,128)}) %all-reduce.2.cloned.1.call-update) | async-done | bytes 3194896 | tf_op jit(solution)/shard_map/psum | solution.py:53
  302.3 3.5 multiply_reduce_fusion
  306.6 0.9 dynamic-slice_multiply_fusion
  307.5 0.6 fusion.7
  308.2 0.6 fusion.5
  308.8 0.6 fusion.3
  309.4 0.6 maximum_bitcast_fusion
  310.0 0.0 all-gather.3.cloned.1.call-update
  310.1 80.3 %all-gather.3.cloned.1.call-done = bf16[128,6,1040]{2,1,0:T(8,128)(2,1)} async-done(((bf16[1,6,1040]{2,1,0:T(8,128)(2,1)}), bf16[128,6,1040]{2,1,0:T(8,128)(2,1)}) %all-gather.3.cloned.1.call-update) | async-done | bytes 1597456 | tf_op jit(solution)/shard_map/all_gather | solution.py:83
  390.3 3.0 reshape.25
  393.3 1.1 slice.27
  394.4 0.8 slice.28
  395.2 0.7 copy.27
  (16 shorter events, 0.0 us)
Async XLA Ops:
  7.2 295.2 %all-reduce.2.cloned.1.call-start = ((), (), s32[]{:S(2)}) async-start(), calls=%async_computation | async-start | bytes 7077888 | tf_op jit(solution)/shard_map/psum | solution.py:53
  13.9 293.6 %copy-start.6 = (f32[6,16]{1,0:T(8,128)S(1)}, f32[6,16]{1,0:T(8,128)}, u32[]{:S(2)}) copy-start(f32[6,16]{1,0:T(8,128)} %param.17) | copy-start | bytes 1156
  13.9 293.6 %copy-start.7 = (f32[6,16]{1,0:T(8,128)S(1)}, f32[6,16]{1,0:T(8,128)}, u32[]{:S(2)}) copy-start(f32[6,16]{1,0:T(8,128)} %param.20) | copy-start | bytes 1156
  13.9 293.6 %copy-start.8 = (f32[6,16]{1,0:T(8,128)S(1)}, f32[6,16]{1,0:T(8,128)}, u32[]{:S(2)}) copy-start(f32[6,16]{1,0:T(8,128)} %param.23) | copy-start | bytes 1156
  13.9 294.2 %copy-start.3 = (f32[6,256]{1,0:T(8,128)S(1)}, f32[6,256]{1,0:T(8,128)}, u32[]{:S(2)}) copy-start(f32[6,256]{1,0:T(8,128)} %param.16) | copy-start | bytes 18436
  13.9 294.2 %copy-start.4 = (f32[6,256]{1,0:T(8,128)S(1)}, f32[6,256]{1,0:T(8,128)}, u32[]{:S(2)}) copy-start(f32[6,256]{1,0:T(8,128)} %param.19) | copy-start | bytes 18436
  13.9 294.2 %copy-start.5 = (f32[6,256]{1,0:T(8,128)S(1)}, f32[6,256]{1,0:T(8,128)}, u32[]{:S(2)}) copy-start(f32[6,256]{1,0:T(8,128)} %param.22) | copy-start | bytes 18436
  13.9 294.8 %copy-start = (f32[6,768]{1,0:T(8,128)S(1)}, f32[6,768]{1,0:T(8,128)}, u32[]{:S(2)}) copy-start(f32[6,768]{1,0:T(8,128)} %param.15) | copy-start | bytes 55300
  13.9 294.8 %copy-start.1 = (f32[6,768]{1,0:T(8,128)S(1)}, f32[6,768]{1,0:T(8,128)}, u32[]{:S(2)}) copy-start(f32[6,768]{1,0:T(8,128)} %param.18) | copy-start | bytes 55300
  14.0 294.8 %copy-start.2 = (f32[6,768]{1,0:T(8,128)S(1)}, f32[6,768]{1,0:T(8,128)}, u32[]{:S(2)}) copy-start(f32[6,768]{1,0:T(8,128)} %param.21) | copy-start | bytes 55300
  14.0 376.3 %all-gather.3.cloned.1.call-start = ((), (), s32[]{:S(2)}) async-start(), calls=%async_computation.1 | async-start | bytes 2377728 | tf_op jit(solution)/shard_map/all_gather | solution.py:83
Sparse Core Ops, SparseCore 0:
  14.1 288.1 all-reduce.1
  310.2 80.0 all-gather.2
where the time goes:
time: 403 us
  waiting for transfers between devices  369 us (92%)
  between operations  14.9 us (4%)
  other arithmetic  13.4 us (3%)
  local copies, waits for them, and re-layouts  5.78 us (1%)
    psum x1, waiting for transfers between devices, body(): full_sum = lax.psum(local_sum, ('dp', 'rep'))  288 us
    all_gather x1, waiting for transfers between devices, body(): collected_parts = lax.all_gather(packed_gradients, 'dp', axis=0, tiled=True)  80.3 us
  transfers between devices with their start and end apart: 2, of which 2 were waited for; matrix products, arithmetic and copies ran while one was open for 0% of the time, Pallas kernels for 0%

commit v1 on v0

--- a/solution.py
+++ b/solution.py
@@ -50,7 +50,9 @@
         ],
         axis=1,
     )
-    full_sum = lax.psum(local_sum, ("dp", "rep"))
+    full_sum = local_sum
+    for name in ("dp", "rep"):
+        full_sum = lax.psum(full_sum, name)
     square_sum = jnp.sum(full_sum * full_sum)
     owned_rows = lax.dynamic_slice_in_dim(full_sum, lax.axis_index("dp") * row_count, row_count, 0)
     clipping_ratio = jnp.minimum(1.0, max_norm / (jnp.sqrt(square_sum) + norm_eps))

time: 403 us -> 420 us (1.042)
  waiting for transfers between devices: 369 us -> 386 us
    psum x1 -> x2, waiting for transfers between devices: 288 us -> 302 us  [body(): full_sum = lax.psum(full_sum, name)]
  transfers between devices with their start and end apart: 2 -> 3, of which waited for: 2 -> 3; matrix products, arithmetic and copies ran while one was open for 0% -> 0% of each run, Pallas kernels for 0% -> 0%
where the time goes in v1:
time: 420 us
  waiting for transfers between devices  386 us (92%)
  between operations  14.6 us (3%)
  other arithmetic  13.4 us (3%)
  local copies, waits for them, and re-layouts  5.78 us (1%)
    psum x2, waiting for transfers between devices, body(): full_sum = lax.psum(full_sum, name)  302 us
    all_gather x1, waiting for transfers between devices, body(): collected_parts = lax.all_gather(packed_gradients, 'dp', axis=0, tiled=True)  83.7 us
  transfers between devices with their start and end apart: 3, of which 3 were waited for; matrix products, arithmetic and copies ran while one was open for 0% of the time, Pallas kernels for 0%

profile of v1, /device:TPU:1, one launch (start us, length us, event | category | flops | bytes accessed | tf_op | source)
XLA Modules:
  0.0 420.1 jit_solution(16020408282837141847)
XLA Ops:
  7.2 0.0 all-reduce.3.cloned.1.call-start
  7.2 0.8 convert_reduce_fusion.2
  8.0 0.2 copy.26
  8.2 1.3 convert_reduce_fusion.1
  9.5 2.3 convert_reduce_fusion
  11.9 2.0 pad_maximum_fusion
  13.9 0.0 all-reduce.3.cloned.1.call-update
  13.9 0.0 all-reduce.5.cloned.1.call-start
  14.0 209.4 %all-reduce.3.cloned.1.call-done = f32[768,1040]{1,0:T(8,128)} async-done(((f32[768,1040]{1,0:T(8,128)}), f32[768,1040]{1,0:T(8,128)}) %all-reduce.3.cloned.1.call-update) | async-done | bytes 3194896 | tf_op jit(solution)/shard_map/psum | solution.py:55
  223.4 0.0 all-reduce.5.cloned.1.call-update
  223.4 0.0 all-gather.3.cloned.1.call-start
  223.5 93.0 %all-reduce.5.cloned.1.call-done = f32[768,1040]{1,0:T(8,128)} async-done(((f32[768,1040]{1,0:T(8,128)}), f32[768,1040]{1,0:T(8,128)}) %all-reduce.5.cloned.1.call-update) | async-done | bytes 3194896 | tf_op jit(solution)/shard_map/psum | solution.py:55
  316.5 3.5 multiply_reduce_fusion
  320.8 0.9 dynamic-slice_multiply_fusion
  321.7 0.6 fusion.7
  322.3 0.6 fusion.5
  323.0 0.6 fusion.3
  323.6 0.6 maximum_bitcast_fusion
  324.2 0.0 all-gather.3.cloned.1.call-update
  324.2 83.7 %all-gather.3.cloned.1.call-done = bf16[128,6,1040]{2,1,0:T(8,128)(2,1)} async-done(((bf16[1,6,1040]{2,1,0:T(8,128)(2,1)}), bf16[128,6,1040]{2,1,0:T(8,128)(2,1)}) %all-gather.3.cloned.1.call-update) | async-done | bytes 1597456 | tf_op jit(solution)/shard_map/all_gather | solution.py:85
  408.0 3.0 reshape.25
  411.0 1.1 slice.27
  412.1 0.8 slice.28
  412.8 0.7 copy.27
  (19 shorter events, 0.1 us)
Async XLA Ops:
  7.2 216.2 %all-reduce.3.cloned.1.call-start = ((), (), s32[]{:S(2)}) async-start(), calls=%async_computation | async-start | bytes 7077888 | tf_op jit(solution)/shard_map/psum | solution.py:55
  13.9 302.6 %all-reduce.5.cloned.1.call-start = ((), (), s32[]{:S(2)}) async-start(), calls=%async_computation.1 | async-start | bytes 7077888 | tf_op jit(solution)/shard_map/psum | solution.py:55
  223.3 98.3 %copy-start.6 = (f32[6,16]{1,0:T(8,128)S(1)}, f32[6,16]{1,0:T(8,128)}, u32[]{:S(2)}) copy-start(f32[6,16]{1,0:T(8,128)} %param.17) | copy-start | bytes 1156
  223.3 98.3 %copy-start.7 = (f32[6,16]{1,0:T(8,128)S(1)}, f32[6,16]{1,0:T(8,128)}, u32[]{:S(2)}) copy-start(f32[6,16]{1,0:T(8,128)} %param.20) | copy-start | bytes 1156
  223.3 98.3 %copy-start.8 = (f32[6,16]{1,0:T(8,128)S(1)}, f32[6,16]{1,0:T(8,128)}, u32[]{:S(2)}) copy-start(f32[6,16]{1,0:T(8,128)} %param.23) | copy-start | bytes 1156
  223.3 99.0 %copy-start.3 = (f32[6,256]{1,0:T(8,128)S(1)}, f32[6,256]{1,0:T(8,128)}, u32[]{:S(2)}) copy-start(f32[6,256]{1,0:T(8,128)} %param.16) | copy-start | bytes 18436
  223.4 99.0 %copy-start.4 = (f32[6,256]{1,0:T(8,128)S(1)}, f32[6,256]{1,0:T(8,128)}, u32[]{:S(2)}) copy-start(f32[6,256]{1,0:T(8,128)} %param.19) | copy-start | bytes 18436
  223.4 99.0 %copy-start.5 = (f32[6,256]{1,0:T(8,128)S(1)}, f32[6,256]{1,0:T(8,128)}, u32[]{:S(2)}) copy-start(f32[6,256]{1,0:T(8,128)} %param.22) | copy-start | bytes 18436
  223.4 99.6 %copy-start = (f32[6,768]{1,0:T(8,128)S(1)}, f32[6,768]{1,0:T(8,128)}, u32[]{:S(2)}) copy-start(f32[6,768]{1,0:T(8,128)} %param.15) | copy-start | bytes 55300
  223.4 99.6 %copy-start.1 = (f32[6,768]{1,0:T(8,128)S(1)}, f32[6,768]{1,0:T(8,128)}, u32[]{:S(2)}) copy-start(f32[6,768]{1,0:T(8,128)} %param.18) | copy-start | bytes 55300
  223.4 99.6 %copy-start.2 = (f32[6,768]{1,0:T(8,128)S(1)}, f32[6,768]{1,0:T(8,128)}, u32[]{:S(2)}) copy-start(f32[6,768]{1,0:T(8,128)} %param.21) | copy-start | bytes 55300
  223.4 184.6 %all-gather.3.cloned.1.call-start = ((), (), s32[]{:S(2)}) async-start(), calls=%async_computation.2 | async-start | bytes 2377728 | tf_op jit(solution)/shard_map/all_gather | solution.py:85
Sparse Core Ops, SparseCore 0:
  14.0 209.2 all-reduce.2
  225.7 90.7 all-reduce.4
  324.4 83.5 all-gather.2
